TPU v7x, 32 devices: a whole 2x2x4 slice. The times are simulated.
32 devices in a mesh: phase: 4 (over y, core), row: 8 (over z, x).
Axes of the slice: x: 2, y: 2, z: 4, core: 2. Of those that a mesh axis runs over, the one named last changes fastest.
Arguments:
- linkage: float32 [2, 4, 1024, 1024], P(None, 'phase', 'row'), as said below
- pulse: float32 [32, 5, 3], replicated, may hold values from -1.2 to 1.2
- segments: int32 [4, 2], P('phase'), may hold values from 0 to 31
- ticks: int32 [4, 2], P('phase'), may hold values from 1 to 4
- detuning: float32 [5], replicated, may hold values from -0.4 to 0.4
- level_shift: float32 [5], replicated, may hold values from -1 to 1
- coupling: float32 [4], replicated, may hold values from -0.5 to 0.5
- dephase: float32 [5], replicated, may hold values from 0.01 to 0.1
Outputs:
- link_gradient: float32 [2, 4, 1024, 1024], P(None, 'phase', 'row')
Inputs may be any that keep to these rules, and one draw needn't show every extreme that they name: Every linkage state is Hermitian: for each phase, the real part is a symmetric matrix and the imaginary part an antisymmetric one.
All inputs are finite; a program needn't handle non-finite values.
Results may differ from a plain program's by a relative error of at most 0.0003.
Values sent between devices are 32-bit elements; how exact they have to be, the bound alone decides.
A program may use at most 64 MiB of HBM per device.

v0:
```python
import functools
import math

import jax
import jax.numpy as jnp
from jax import lax
from jax.experimental import pallas as pl
from jax.experimental.pallas import tpu as pltpu
from jax.sharding import PartitionSpec as P

TRANSMONS = 5
LEVELS = 4
STEPS = 2
SEGMENTS = 32
HALF = 2
MESH = pl.DeviceIdType.MESH


TOP_ACCURACY = lax.Precision.HIGHEST


def prefix(value, axis, join, neutral):
    count, mine = (lax.axis_size(axis), lax.axis_index(axis))
    pieces = lax.all_gather(value, axis)
    subtotal = jnp.full_like(value, 0) + jnp.asarray(neutral, value.dtype)

    def lap(position, subtotal):
        longer = join(subtotal, pieces[position])
        return jnp.where(position < mine, longer, subtotal)

    return lax.fori_loop(0, count - 1, lap, subtotal)


def shifted(block, axis, distance):
    devices = range(lax.axis_size(axis))
    route = [((i - distance) % len(devices), i) for i in devices]
    return lax.ppermute(block, axis, route)


def digits(indices):
    powers = LEVELS ** (TRANSMONS - 1 - jnp.arange(TRANSMONS, dtype=jnp.int32))
    return (indices[None, :] // powers[:, None] % LEVELS).astype(jnp.float32)


def energies(levels, level_shift, coupling):
    own_part = jnp.sum(level_shift[:, None] * levels * (levels - 1.0) * 0.5, axis=0)
    return own_part + jnp.sum(coupling[:, None] * levels[:-1] * levels[1:], axis=0)


def drift_tables(row_levels, col_levels, level_shift, coupling, dephase):
    detune_grid = (
        energies(row_levels, level_shift, coupling)[:, None]
        - energies(col_levels, level_shift, coupling)[None, :]
    )
    weighted = dephase[:, None] * row_levels
    cross = jnp.dot(
        weighted.T, col_levels, preferred_element_type=jnp.float32, precision=TOP_ACCURACY
    )
    row_part = jnp.sum(weighted * row_levels, axis=0)
    col_part = jnp.sum(dephase[:, None] * col_levels * col_levels, axis=0)
    decay = row_part[:, None] + col_part[None, :] - 2.0 * cross
    return (decay, detune_grid)


def half_factor(decay, detune_grid, span):
    magnitude = jnp.exp(-0.5 * span * decay)
    return (
        magnitude * jnp.cos(0.5 * span * detune_grid),
        -magnitude * jnp.sin(0.5 * span * detune_grid),
    )


def weigh(field, factor_real, factor_imag):
    return jnp.stack(
        [
            field[0] * factor_real - field[1] * factor_imag,
            field[0] * factor_imag + field[1] * factor_real,
        ]
    )


def complex_product(left_real_component, left_imaginary, right_real_component, right_imaginary):
    real_component = jnp.einsum(
        "nmx,nxw->nmw", left_real_component, right_real_component, precision=TOP_ACCURACY
    ) - jnp.einsum("nmx,nxw->nmw", left_imaginary, right_imaginary, precision=TOP_ACCURACY)
    imaginary_component = jnp.einsum(
        "nmx,nxw->nmw", left_real_component, right_imaginary, precision=TOP_ACCURACY
    ) + jnp.einsum("nmx,nxw->nmw", left_imaginary, right_real_component, precision=TOP_ACCURACY)
    return (real_component, imaginary_component)


def rotations(theta, phi):
    identity = jnp.eye(LEVELS, dtype=jnp.float32)
    total_real = jnp.broadcast_to(identity, (theta.shape[0], LEVELS, LEVELS))
    total_imag = jnp.zeros((theta.shape[0], LEVELS, LEVELS), jnp.float32)
    for level in range(LEVELS - 1):
        upper = jnp.outer(identity[level], identity[level + 1])
        lower = upper.T
        block = jnp.outer(identity[level], identity[level]) + jnp.outer(
            identity[level + 1], identity[level + 1]
        )
        cosine = jnp.cos(theta[:, level])[:, None, None]
        sine = jnp.sin(theta[:, level])[:, None, None]
        phase_cos = jnp.cos(phi[:, level])[:, None, None]
        phase_sin = jnp.sin(phi[:, level])[:, None, None]
        rot_real = identity + (cosine - 1.0) * block + sine * phase_cos * (lower - upper)
        rot_imag = sine * phase_sin * (upper + lower)
        total_real, total_imag = complex_product(total_real, total_imag, rot_real, rot_imag)
    return (total_real, total_imag)


def kron_range(unit_real, unit_imag, first, last):
    acc_real, acc_imag = (unit_real[first], unit_imag[first])
    for transmon in range(first + 1, last):
        next_real, next_imag = (unit_real[transmon], unit_imag[transmon])
        acc_real, acc_imag = (
            jnp.kron(acc_real, next_real) - jnp.kron(acc_imag, next_imag),
            jnp.kron(acc_real, next_imag) + jnp.kron(acc_imag, next_real),
        )
    return (acc_real, acc_imag)


def real_form(matrix_real, matrix_imag):
    return jnp.stack(
        [
            jnp.stack([matrix_real, -matrix_imag], axis=1),
            jnp.stack([matrix_imag, matrix_real], axis=1),
        ],
        axis=0,
    )


def factor_forms(unit_real, unit_imag):
    pairs = [
        kron_range(unit_real, unit_imag, 0, HALF),
        kron_range(unit_real, unit_imag, HALF, TRANSMONS),
    ]
    forward_left = [real_form(matrix_real, matrix_imag) for matrix_real, matrix_imag in pairs]
    forward_right = [real_form(matrix_real, -matrix_imag) for matrix_real, matrix_imag in pairs]
    adjoint_left = [real_form(matrix_real.T, -matrix_imag.T) for matrix_real, matrix_imag in pairs]
    adjoint_right = [real_form(matrix_real.T, matrix_imag.T) for matrix_real, matrix_imag in pairs]
    return (forward_left, forward_right, adjoint_left, adjoint_right)


def apply_factor(field, form, leading, trailing):
    width = form.shape[3]
    shaped = field.reshape(2, leading, width, trailing)
    result = jnp.einsum("cgdf,dpfq->cpgq", form, shaped, precision=TOP_ACCURACY)
    return result.reshape(field.shape)


def apply_factors(field, forms, leading, trailing):
    widths = [form.shape[3] for form in forms]
    for position, form in enumerate(forms):
        before = math.prod(widths[:position])
        after = math.prod(widths[position + 1 :])
        field = apply_factor(field, form, leading * before, after * trailing)
    return field


def step_unitaries(pulse, segment, clock, span, detuning):
    onehot = (jnp.arange(SEGMENTS, dtype=jnp.int32) == segment).astype(jnp.float32)
    theta = jnp.einsum("s,skm->km", onehot, pulse, precision=TOP_ACCURACY)
    multiple = jnp.arange(1, LEVELS, dtype=jnp.int32).astype(jnp.float32)
    phi = detuning[:, None] * (clock + 0.5 * span) * multiple[None, :]
    return rotations(theta, phi)


def sandwich(field, left_forms, right_forms):
    local_rows = field.shape[1]
    order_size = field.shape[2]
    members = lax.axis_size("row")
    block_width = order_size // members
    halfway = apply_factors(field, right_forms, local_rows, 1)
    halfway = halfway.reshape(2, local_rows, members, block_width)
    received = lax.all_to_all(halfway, "row", split_axis=2, concat_axis=1, tiled=True)
    count = received.shape[3]
    columns = apply_factors(received.reshape(2, order_size, count), left_forms, 1, count)
    turned = jnp.stack([columns[0].T, -columns[1].T])
    result = turned.reshape(2, 1, count, order_size)
    return result.reshape(2, block_width, order_size)


def local(linkage, pulse, segments, ticks, detuning, level_shift, coupling, dephase):
    current = linkage[:, 0]
    local_rows = current.shape[1]
    order_size = current.shape[2]
    row_rank = lax.axis_index("row")
    row_levels = digits(row_rank * local_rows + jnp.arange(local_rows, dtype=jnp.int32))
    col_levels = digits(jnp.arange(order_size, dtype=jnp.int32))
    decay, detune_grid = drift_tables(row_levels, col_levels, level_shift, coupling, dephase)
    step_ticks = ticks[0]

    def add_ticks(earlier, later):
        return earlier + later

    offsets = prefix(
        jnp.sum(step_ticks, keepdims=True, dtype=jnp.int32),
        "phase",
        add_ticks,
        jnp.zeros((1,), jnp.int32),
    )
    prepared = []
    for step_index in range(STEPS):
        span = step_ticks[step_index].astype(jnp.float32)
        clock = (offsets[0] + jnp.sum(step_ticks[:step_index], dtype=jnp.int32)).astype(jnp.float32)
        unit_real, unit_imag = step_unitaries(pulse, segments[0, step_index], clock, span, detuning)
        factor_real, factor_imag = half_factor(decay, detune_grid, span)
        prepared.append((factor_real, factor_imag, factor_forms(unit_real, unit_imag)))
    following = shifted(current, "phase", -1)
    field = current
    for forward_step_index in range(STEPS):
        forward_factor_real, forward_factor_imag, forward_forms = prepared[forward_step_index]
        field = weigh(field, forward_factor_real, forward_factor_imag)
        field = sandwich(field, forward_forms[0], forward_forms[1])
        field = weigh(field, forward_factor_real, forward_factor_imag)
    mismatch = field - following
    earlier_mismatch = shifted(mismatch, "phase", 1)
    adjoint = mismatch
    for step_index in reversed(range(STEPS)):
        factor_real, factor_imag, forms = prepared[step_index]
        adjoint = weigh(adjoint, factor_real, -factor_imag)
        adjoint = sandwich(adjoint, forms[2], forms[3])
        adjoint = weigh(adjoint, factor_real, -factor_imag)
    return (adjoint - earlier_mismatch)[:, None]


def table_slots():
    quads = STEPS * TRANSMONS * LEVELS * LEVELS
    names = [("q", quads), ("w", STEPS * TRANSMONS), ("t", STEPS), ("e", TRANSMONS)]
    names += [("c", TRANSMONS - 1), ("d", TRANSMONS)]
    slots, offset = {}, 0
    for name, count in names:
        slots[name] = offset
        offset += count
    return slots


def dot3(left_high, left_low, right_high, right_low, contract_right=0):
    dims = (((1,), (contract_right,)), ((), ()))

    def one(left, right):
        return lax.dot_general(left, right, dims, preferred_element_type=jnp.float32)

    return one(left_high, right_high) + (one(left_high, right_low) + one(left_low, right_high))


def split(value):
    high = value.astype(jnp.bfloat16)
    return high, (value - high.astype(jnp.float32)).astype(jnp.bfloat16)


def kernel(
    phases,
    members,
    scalars,
    state,
    out,
    following,
    mismatch,
    earlier,
    first_high,
    first_low,
    second_high,
    second_low,
    sides,
    pre_table,
    mid_table,
    post_table,
    turned,
    gathered_high,
    gathered_low,
    halfway,
    send_one,
    receive_one,
    send_two,
    receive_two,
    send_sems,
    receive_sems,
    phase_sems,
    own_sems,
):
    phase = lax.axis_index("phase")
    me = lax.axis_index("row")
    rows, order = state.shape[1], state.shape[2]
    lead = LEVELS**HALF
    trail = order // lead
    count = trail // members
    lanes = lead * count
    per = lead // members
    slots = table_slots()

    def q(step, k, i, j):
        return scalars[slots["q"] + ((step * TRANSMONS + k) * LEVELS + i) * LEVELS + j]

    def digit(index, k):
        return (index >> (2 * (TRANSMONS - 1 - k))) & (LEVELS - 1)

    barrier = pltpu.get_barrier_semaphore()
    after, before = lax.rem(phase + 1, phases), lax.rem(phase + phases - 1, phases)
    for offset in range(1, members):
        peer = lax.rem(me + offset, members)
        pl.semaphore_signal(barrier, inc=1, device_id=(phase, peer), device_id_type=MESH)
    for peer in (after, before):
        pl.semaphore_signal(barrier, inc=1, device_id=(peer, me), device_id_type=MESH)

    def pick(index, k, values):
        place = digit(index, k)
        result = jnp.where(place == 0, values[0], values[1])
        result = jnp.where(place == 2, values[2], result)
        return jnp.where(place == 3, values[3], result)

    def entries(row_index, col_index, k, step, swapped):
        vectors = []
        for i in range(LEVELS):
            values = [q(step, k, j, i) if swapped else q(step, k, i, j) for j in range(LEVELS)]
            vectors.append(pick(col_index, k, values))
        return pick(row_index, k, vectors)

    def kron_entries(row_index, col_index, ks, step, swapped):
        result = entries(row_index, col_index, ks[0], step, swapped)
        for k in ks[1:]:
            result = result * entries(row_index, col_index, k, step, swapped)
        return result

    head, tail = range(HALF), range(HALF, TRANSMONS)

    def iota(shape, axis):
        return lax.broadcasted_iota(jnp.int32, shape, axis)

    def build_dense(high, low, step, swapped):
        lane = iota((1, lanes), 1)
        lead_rows = [
            kron_entries(
                jnp.full((1, 1), a * trail, jnp.int32), (lane // count) * trail, head, step, swapped
            )
            for a in range(lead)
        ]
        for block in range(members):
            tile = kron_entries(
                iota((trail, 1), 0), block * count + lane % count, tail, step, swapped
            )
            for a in range(lead):
                upper, lower = split(tile * lead_rows[a])
                where = (slice(a * trail, (a + 1) * trail), slice(block * lanes, (block + 1) * lanes))
                high[where] = upper
                low[where] = lower

    def build_sides(step):
        row, col = iota((rows, 1), 0), iota((1, rows), 1)
        same = (row // trail) == (col // trail)
        lrow, lcol = iota((lanes, 1), 0), iota((1, lanes), 1)
        aligned = (lrow % count) == (lcol % count)
        for swapped in (False, True):
            body = kron_entries(row % trail, col % trail, tail, step, swapped)
            upper, lower = split(jnp.where(same, body, 0.0))
            base = 8 * step + 4 * swapped
            sides[base] = upper
            sides[base + 1] = lower
            body = kron_entries(
                (lrow // count) * trail, (lcol // count) * trail, head, step, swapped
            )
            upper, lower = split(jnp.where(aligned, body, 0.0))
            sides[base + 2] = upper
            sides[base + 3] = lower

    tau = [scalars[slots["t"] + s] for s in range(STEPS)]

    def angle(index, which):
        n = [digit(index, k).astype(jnp.float32) for k in range(TRANSMONS)]
        energy = jnp.zeros(index.shape, jnp.float32)
        for k in range(TRANSMONS):
            energy = energy + scalars[slots["e"] + k] * (n[k] * (n[k] - 1.0) * 0.5)
        for k in range(TRANSMONS - 1):
            energy = energy + scalars[slots["c"] + k] * (n[k] * n[k + 1])
        triangle = [v * (v + 1.0) * 0.5 for v in n]
        spin = [
            sum(scalars[slots["w"] + s * TRANSMONS + k] * triangle[k] for k in range(TRANSMONS))
            for s in range(STEPS)
        ]
        if which == 0:
            return -spin[0] - 0.5 * tau[0] * energy
        if which == 1:
            return (spin[0] - spin[1]) - 0.5 * (tau[0] + tau[1]) * energy
        return spin[1] - 0.5 * tau[1] * energy

    spans = (tau[0], tau[0] + tau[1], tau[1])

    def waves(index, which):
        value = angle(index, which)
        return jnp.cos(value), jnp.sin(value)

    def factor(row_index, col_index, row_waves, col_waves, which):
        decay = 0.0
        for k in range(TRANSMONS):
            gap = digit(row_index, k).astype(jnp.float32) - digit(col_index, k).astype(jnp.float32)
            decay = decay + scalars[slots["d"] + k] * (gap * gap)
        size = jnp.exp(-0.5 * spans[which] * decay)
        row_cos, row_sin = row_waves
        col_cos, col_sin = col_waves
        return (
            size * (row_cos * col_cos + row_sin * col_sin),
            size * (row_sin * col_cos - row_cos * col_sin),
        )

    width = 128

    def build_row_table(table, which):
        row = me * rows + iota((rows, 1), 0)
        row_waves = waves(row, which)
        for chunk in range(order // width):
            col = chunk * width + iota((1, width), 1)
            real, imag = factor(row, col, row_waves, waves(col, which), which)
            table[0, :, pl.ds(chunk * width, width)] = real
            table[1, :, pl.ds(chunk * width, width)] = imag

    def build_mid_table():
        for block in range(members):
            other = lax.rem(me + members - block, members)
            lrow, lane = iota((lanes, 1), 0), iota((1, lanes), 1)
            row = (lrow // count) * trail + block * count + lrow % count
            col = (lane // count) * trail + other * count + lane % count
            real, imag = factor(row, col, waves(row, 1), waves(col, 1), 1)
            mid_table[0, block] = real
            mid_table[1, block] = imag

    def exchange(source, target, trip):
        copies = []
        for offset in range(1, members):
            peer = lax.rem(me + offset, members)
            copy = pltpu.make_async_remote_copy(
                src_ref=source.at[peer],
                dst_ref=target.at[me],
                send_sem=send_sems.at[trip, offset],
                recv_sem=receive_sems.at[trip, offset],
                device_id=(phase, peer),
                device_id_type=MESH,
            )
            copy.start()
            copies.append(copy)
        own = pltpu.make_async_copy(source.at[me], target.at[me], own_sems.at[trip])
        own.start()
        copies.append(own)
        return copies

    def hand(source, target, peer, number):
        copy = pltpu.make_async_remote_copy(
            src_ref=source,
            dst_ref=target,
            send_sem=phase_sems.at[0, number],
            recv_sem=phase_sems.at[1, number],
            device_id=(peer, me),
            device_id_type=MESH,
        )
        copy.start()
        return copy

    def outbound(read, sign, table, side, high, low, trip):
        left_high, left_low = sides[side], sides[side + 1]
        for chunk in range(order // width):
            where = pl.ds(chunk * width, width)
            straight, crossed = read(where)
            value = table[0, :, where] * straight + sign * (table[1, :, where] * crossed)
            moved = dot3(left_high, left_low, *split(value))
            upper, lower = split(moved)
            gathered_high[0:rows, where] = upper
            gathered_low[0:rows, where] = lower
        pack = 2
        for pair in range(members // pack):
            where = pl.ds(pair * pack * lanes, pack * lanes)
            moved = dot3(
                gathered_high[0:rows, :], gathered_low[0:rows, :], high[:, where], low[:, where]
            )
            for inner in range(pack):
                block = pair * pack + inner
                for b in range(members):
                    for part in range(per):
                        start = part * trail + b * count
                        send_one[trip // 2, (b + block) % members, start : start + count, :] = moved[
                            start : start + count, inner * lanes : (inner + 1) * lanes
                        ]
        return exchange(send_one.at[trip // 2], receive_one.at[trip // 2], trip)

    def middle(sign, first_side, second_side, trip):
        went = trip // 2
        for block in range(members):
            pieces = []
            for a in range(lead):
                start = (a % per) * trail + block * count
                pieces.append(receive_one[went, a // per, start : start + count, :])
            value = jnp.concatenate(pieces, axis=0)
            turned[block] = dot3(sides[first_side], sides[first_side + 1], *split(value))
        for block in range(members):
            other = lax.rem(me + members - block, members)
            straight = turned[block]
            crossed = turned[other].T
            real, imag = mid_table[0, block], sign * mid_table[1, block]
            for kind, value in enumerate(
                (real * straight + imag * crossed, real * crossed - imag * straight)
            ):
                moved = dot3(sides[second_side], sides[second_side + 1], *split(value))
                for a in range(lead):
                    start = (a % per) * trail + block * count
                    send_two[went, a // per, kind, start : start + count, :] = moved[
                        a * count : (a + 1) * count, :
                    ]
        return exchange(send_two.at[went], receive_two.at[went], trip)

    def inbound(side, high, low, trip):
        went = trip // 2
        for block in range(members):
            for kind in range(2):
                pieces = []
                for part in range(per):
                    for b in range(members):
                        start = part * trail + b * count
                        pieces.append(
                            receive_two[went, (b + block) % members, kind, start : start + count, :]
                        )
                upper, lower = split(jnp.concatenate(pieces, axis=0))
                where = (slice(kind * rows, (kind + 1) * rows), slice(block * lanes, (block + 1) * lanes))
                gathered_high[where] = upper
                gathered_low[where] = lower
        wide = 2 * width
        for chunk in range(order // wide):
            where = pl.ds(chunk * wide, wide)
            moved = dot3(gathered_high[...], gathered_low[...], high[where, :], low[where, :], 1)
            for kind in range(2):
                halfway[kind, :, where] = dot3(
                    sides[side], sides[side + 1], *split(moved[kind * rows : (kind + 1) * rows])
                )

    def wait(copies):
        for copy in copies:
            copy.wait()

    build_row_table(pre_table, 0)
    build_dense(first_high, first_low, 0, True)
    build_sides(0)
    pl.semaphore_wait(barrier, members + 1)

    def read_state(where):
        real, imag = state[0, :, where], state[1, :, where]
        return real + imag, real - imag

    copies = outbound(read_state, 1.0, pre_table, 0, first_high, first_low, 0)
    handed = hand(state, following, before, 0)
    build_sides(1)
    build_mid_table()
    build_dense(second_high, second_low, 1, False)
    build_row_table(post_table, 2)
    wait(copies)
    copies = middle(1.0, 2, 10, 1)
    handed.wait()
    wait(copies)
    inbound(8, second_high, second_low, 1)
    for chunk in range(order // width):
        where = pl.ds(chunk * width, width)
        straight, crossed = halfway[0, :, where], halfway[1, :, where]
        real, imag = post_table[0, :, where], post_table[1, :, where]
        next_real, next_imag = following[0, :, where], following[1, :, where]
        mismatch[0, :, where] = real * straight + imag * crossed - (next_real + next_imag)
        mismatch[1, :, where] = real * crossed - imag * straight - (next_real - next_imag)

    def read_mismatch(where):
        return mismatch[0, :, where], mismatch[1, :, where]

    copies = outbound(read_mismatch, -1.0, post_table, 12, second_high, second_low, 2)
    handed = hand(mismatch, earlier, after, 1)
    wait(copies)
    copies = middle(-1.0, 14, 6, 3)
    handed.wait()
    wait(copies)
    inbound(4, first_high, first_low, 3)
    for chunk in range(order // width):
        where = pl.ds(chunk * width, width)
        straight, crossed = halfway[0, :, where], halfway[1, :, where]
        real, imag = pre_table[0, :, where], -pre_table[1, :, where]
        upper = real * straight + imag * crossed - earlier[0, :, where]
        lower = real * crossed - imag * straight - earlier[1, :, where]
        out[0, :, where] = 0.5 * (upper + lower)
        out[1, :, where] = 0.5 * (upper - lower)


def fused(linkage, pulse, segments, ticks, detuning, level_shift, coupling, dephase):
    phases, members = lax.axis_size("phase"), lax.axis_size("row")
    current = linkage[:, 0]
    rows, order = current.shape[1], current.shape[2]
    mine = lax.axis_index("phase")
    total = jnp.sum(ticks, axis=1, dtype=jnp.int32)
    start = jnp.zeros((1,), jnp.int32)
    for distance in range(1, phases):
        other = shifted(total, "phase", distance)
        start = start + jnp.where(mine >= distance, other, 0)
    tau = ticks[0].astype(jnp.float32)
    clock = (start + jnp.cumsum(ticks[0]) - ticks[0]).astype(jnp.float32)
    spin = (clock + 0.5 * tau)[:, None] * detuning[None, :]
    onehot = (segments[0][:, None] == jnp.arange(SEGMENTS, dtype=jnp.int32)[None, :])
    theta = jnp.sum(jnp.where(onehot[:, :, None, None], pulse[None], 0.0), axis=1)
    cosine, sine = jnp.cos(theta), jnp.sin(theta)
    one = jnp.ones_like(cosine[:, :, 0])
    cells = []
    for i in range(LEVELS):
        for j in range(LEVELS):
            if i > j + 1:
                cells.append(0.0 * one)
            elif i == j + 1:
                cells.append(sine[:, :, j])
            else:
                cell = one if i == 0 else cosine[:, :, i - 1]
                for m in range(i, j):
                    cell = cell * -sine[:, :, m]
                cells.append(cell if j == LEVELS - 1 else cell * cosine[:, :, j])
    quads = jnp.stack(cells, axis=-1)
    scalars = jnp.concatenate(
        [quads.reshape(-1), spin.reshape(-1), tau, level_shift, coupling, dephase]
    )
    lanes = order // members
    full = (2, rows, order)
    one_way = (2, members, rows, lanes)
    two_way = (2, members, 2, rows, lanes)
    vmem = pl.BlockSpec(memory_space=pltpu.VMEM)
    result = pl.pallas_call(
        functools.partial(kernel, phases, members),
        out_shape=jax.ShapeDtypeStruct(full, jnp.float32),
        in_specs=[pl.BlockSpec(memory_space=pltpu.SMEM), vmem],
        out_specs=vmem,
        scratch_shapes=[
            pltpu.VMEM(full, jnp.float32),
            pltpu.VMEM(full, jnp.float32),
            pltpu.VMEM(full, jnp.float32),
            pltpu.VMEM((order, order), jnp.bfloat16),
            pltpu.VMEM((order, order), jnp.bfloat16),
            pltpu.VMEM((order, order), jnp.bfloat16),
            pltpu.VMEM((order, order), jnp.bfloat16),
            pltpu.VMEM((8 * STEPS, rows, rows), jnp.bfloat16),
            pltpu.VMEM(full, jnp.float32),
            pltpu.VMEM((2, members, lanes, lanes), jnp.float32),
            pltpu.VMEM(full, jnp.float32),
            pltpu.VMEM((members, lanes, lanes), jnp.float32),
            pltpu.VMEM((2 * rows, order), jnp.bfloat16),
            pltpu.VMEM((2 * rows, order), jnp.bfloat16),
            pltpu.VMEM(full, jnp.float32),
            pltpu.VMEM(one_way, jnp.float32),
            pltpu.VMEM(one_way, jnp.float32),
            pltpu.VMEM(two_way, jnp.float32),
            pltpu.VMEM(two_way, jnp.float32),
            pltpu.SemaphoreType.DMA((4, members)),
            pltpu.SemaphoreType.DMA((4, members)),
            pltpu.SemaphoreType.DMA((2, 2)),
            pltpu.SemaphoreType.DMA((4,)),
        ],
        compiler_params=pltpu.CompilerParams(
            collective_id=0, has_side_effects=True, vmem_limit_bytes=56 * 1024 * 1024
        ),
    )(scalars, current)
    return result[:, None]


def solution(mesh):
    members = mesh.shape["row"]
    trail = LEVELS ** (TRANSMONS - HALF)
    fits = STEPS == 2 and members <= LEVELS**HALF and LEVELS**HALF * (trail // members) == 128
    return jax.shard_map(
        fused if fits else local,
        mesh=mesh,
        in_specs=(
            P(None, "phase", "row", None),
            P(),
            P("phase", None),
            P("phase", None),
            P(),
            P(),
            P(),
            P(),
        ),
        out_specs=P(None, "phase", "row", None),
        check_vma=False,
    )
```

profile of v0, /device:TPU:10, one launch (start us, length us, event | category | flops | bytes accessed | tf_op | source)
XLA Modules:
  0.0 105.9 jit_solution(12897026305236039012)
XLA Ops:
  0.0 1.3 %bitcast_convert_fusion = (f32[2]{0:T(128)S(1)}, s32[]{:T(128)}) fusion(s32[1,2]{1,0:T(1,128)} %param.11), kind=kLoop, calls=%fused_computation.7 | loop fusion | flops 3 | bytes 20 | tf_op jit(solution)/shard_map/convert_element_type | solution.py:595
  1.3 1.0 collective-permute-start.2
  2.3 0.6 collective-permute-start.1
  2.8 0.2 collective-permute-start
  3.1 0.7 iota_compare_fusion
  3.8 0.1 select_reduce_fusion
  3.9 0.1 copy.27
  4.0 0.1 fusion.5
  4.1 0.1 copy.41
  4.2 0.1 copy.37
  4.3 0.1 copy.29
  4.4 0.1 copy.34
  4.5 0.1 copy.38
  4.6 0.1 copy.30
  4.7 0.1 copy.35
  4.8 0.1 copy.31
  4.9 0.1 copy.36
  5.0 0.1 copy.39
  5.1 0.1 copy.40
  5.2 0.1 copy.32
  5.3 0.1 copy.33
  5.4 0.1 stack.2
  5.5 0.1 reshape.76
  5.6 0.7 copy-done.4
  6.3 0.2 reduce-window.8
  8.3 0.6 copy-done.5
  8.9 0.1 broadcast_multiply_fusion
  9.0 0.1 mul.82
  9.1 0.6 copy-done.1
  9.8 0.6 concatenate.3.scalars
  10.4 93.1 %shard_map.82 = f32[2,128,1024]{2,1,0:T(8,128)} custom-call(f32[186]{0:T(256)} %concatenate.3.scalars, f32[2,128,1024]{2,1,0:T(8,128)} %bitcast.23), custom_call_target="tpu_custom_call" | custom-call | tf_op jit(solution)/shard_map/pallas_call | solution.py:623
  103.6 2.3 %copy.44 = f32[2,1,128,1024]{3,2,1,0:T(8,128)} copy(f32[2,1,128,1024]{3,2,1,0:T(8,128)} %bitcast.22) | data formatting | bytes 2097152
  (18 shorter events, 0.1 us)
Async XLA Ops:
  0.0 3.8 %copy-start = (f32[32,5,3]{0,2,1:T(4,128)S(1)}, f32[32,5,3]{0,2,1:T(4,128)}, u32[]{:S(2)}) copy-start(f32[32,5,3]{0,2,1:T(4,128)} %param.9) | copy-start | bytes 5764
  1.3 6.4 %collective-permute-start.2 = (s32[1]{0:T(128)}, s32[1]{0:T(128)}, u32[]{:S(2)}, u32[]{:S(2)}) collective-permute-start(s32[1]{0:T(128)} %bitcast.2), channel_id=1, source_target_pairs={{8,0},{16,8},{24,16},{0,24},{9,1},{17,9},{25,17},{1,25},{10,2},{18... | collective-permute-start | bytes 20 | tf_op jit(solution)/shard_map/ppermute | solution.py:37
  2.3 4.2 %collective-permute-start.1 = (s32[1]{0:T(128)}, s32[1]{0:T(128)}, u32[]{:S(2)}, u32[]{:S(2)}) collective-permute-start(s32[1]{0:T(128)} %bitcast.2), channel_id=1, source_target_pairs={{16,0},{24,8},{0,16},{8,24},{17,1},{25,9},{1,17},{9,25},{18,2},{26... | collective-permute-start | bytes 20 | tf_op jit(solution)/shard_map/ppermute | solution.py:37
  2.8 4.3 %collective-permute-start = (s32[1]{0:T(128)}, s32[1]{0:T(128)}, u32[]{:S(2)}, u32[]{:S(2)}) collective-permute-start(s32[1]{0:T(128)} %bitcast.2), channel_id=1, source_target_pairs={{24,0},{0,8},{8,16},{16,24},{25,1},{1,9},{9,17},{17,25},{26,2},{2,... | collective-permute-start | bytes 20 | tf_op jit(solution)/shard_map/ppermute | solution.py:37
  5.6 0.7 copy-start.4
  8.3 0.7 copy-start.5
  9.1 0.7 copy-start.1
  9.1 0.7 copy-start.2
  9.1 0.7 copy-start.3
where the time goes:
time: 106 us
  Pallas kernels  93.1 us (88%)
  local copies, waits for them, and re-layouts  6.65 us (6%)
  other arithmetic  2.4 us (2%)
  between operations  1.91 us (2%)
  starting transfers between devices  1.75 us (2%)
    pallas_call x1, Pallas kernels, fused(): pl.pallas_call(functools.partial(kernel, phases, members), out_shape=jax....  93.1 us
    unnamed x13, local copies, waits for them, and re-layouts  4.3 us
  transfers between devices with their start and end apart: 3, of which 0 were waited for; matrix products, arithmetic and copies ran while one was open for 2% of the time, Pallas kernels for 0%

commit v1 on v0

--- a/solution.py
+++ b/solution.py
@@ -225,17 +225,6 @@
     return (adjoint - earlier_mismatch)[:, None]
 
 
-def table_slots():
-    quads = STEPS * TRANSMONS * LEVELS * LEVELS
-    names = [("q", quads), ("w", STEPS * TRANSMONS), ("t", STEPS), ("e", TRANSMONS)]
-    names += [("c", TRANSMONS - 1), ("d", TRANSMONS)]
-    slots, offset = {}, 0
-    for name, count in names:
-        slots[name] = offset
-        offset += count
-    return slots
-
-
 def dot3(left_high, left_low, right_high, right_low, contract_right=0):
     dims = (((1,), (contract_right,)), ((), ()))
 
@@ -250,12 +239,41 @@
     return high, (value - high.astype(jnp.float32)).astype(jnp.bfloat16)
 
 
+def rotation_cells(cosine, sine, k):
+    def at(table, m):
+        return table[k : k + 1, m : m + 1]
+
+    rows = []
+    for i in range(LEVELS):
+        row = []
+        for j in range(LEVELS):
+            if i > j + 1:
+                row.append(jnp.zeros((1, 1), jnp.float32))
+            elif i == j + 1:
+                row.append(at(sine, j))
+            else:
+                factors = [] if i == 0 else [at(cosine, i - 1)]
+                factors += [-at(sine, m) for m in range(i, j)]
+                factors += [] if j == LEVELS - 1 else [at(cosine, j)]
+                row.append(math.prod(factors[1:], start=factors[0]))
+        rows.append(row)
+    return rows
+
+
 def kernel(
     phases,
     members,
-    scalars,
+    ticks,
+    segments,
+    detuning,
+    level_shift,
+    coupling,
+    dephase,
+    tick_row,
+    pulse,
     state,
     out,
+    tick_rows,
     following,
     mismatch,
     earlier,
@@ -279,6 +297,7 @@
     receive_sems,
     phase_sems,
     own_sems,
+    tick_sems,
 ):
     phase = lax.axis_index("phase")
     me = lax.axis_index("row")
@@ -288,10 +307,14 @@
     count = trail // members
     lanes = lead * count
     per = lead // members
-    slots = table_slots()
+    cells = []
+    for step in range(STEPS):
+        theta = pulse[segments[0, step]]
+        cosine, sine = jnp.cos(theta), jnp.sin(theta)
+        cells.append([rotation_cells(cosine, sine, k) for k in range(TRANSMONS)])
 
     def q(step, k, i, j):
-        return scalars[slots["q"] + ((step * TRANSMONS + k) * LEVELS + i) * LEVELS + j]
+        return cells[step][k][i][j]
 
     def digit(index, k):
         return (index >> (2 * (TRANSMONS - 1 - k))) & (LEVELS - 1)
@@ -301,7 +324,8 @@
     for offset in range(1, members):
         peer = lax.rem(me + offset, members)
         pl.semaphore_signal(barrier, inc=1, device_id=(phase, peer), device_id_type=MESH)
-    for peer in (after, before):
+    for distance in range(1, phases):
+        peer = lax.rem(phase + distance, phases)
         pl.semaphore_signal(barrier, inc=1, device_id=(peer, me), device_id_type=MESH)
 
     def pick(index, k, values):
@@ -364,18 +388,46 @@
             sides[base + 2] = upper
             sides[base + 3] = lower
 
-    tau = [scalars[slots["t"] + s] for s in range(STEPS)]
+    tau = [ticks[0, s].astype(jnp.float32) for s in range(STEPS)]
+
+    def send_ticks():
+        copies = []
+        for distance in range(1, phases):
+            copy = pltpu.make_async_remote_copy(
+                src_ref=tick_row,
+                dst_ref=tick_rows.at[phase],
+                send_sem=tick_sems.at[0, distance],
+                recv_sem=tick_sems.at[1, distance],
+                device_id=(lax.rem(phase + distance, phases), me),
+                device_id_type=MESH,
+            )
+            copy.start()
+            copies.append(copy)
+        return copies
+
+    weights = []
+
+    def set_weights():
+        start = jnp.zeros((1, 1), jnp.int32)
+        for distance in range(1, phases):
+            row = tick_rows[lax.rem(phase + phases - distance, phases)]
+            total = sum(row[:, s : s + 1] for s in range(STEPS))
+            start = start + jnp.where(phase >= distance, total, 0)
+        for s in range(STEPS):
+            clock = start.astype(jnp.float32)
+            weights.append([(clock + 0.5 * tau[s]) * detuning[k] for k in range(TRANSMONS)])
+            start = start + ticks[0, s]
 
     def angle(index, which):
         n = [digit(index, k).astype(jnp.float32) for k in range(TRANSMONS)]
         energy = jnp.zeros(index.shape, jnp.float32)
         for k in range(TRANSMONS):
-            energy = energy + scalars[slots["e"] + k] * (n[k] * (n[k] - 1.0) * 0.5)
+            energy = energy + level_shift[k] * (n[k] * (n[k] - 1.0) * 0.5)
         for k in range(TRANSMONS - 1):
-            energy = energy + scalars[slots["c"] + k] * (n[k] * n[k + 1])
+            energy = energy + coupling[k] * (n[k] * n[k + 1])
         triangle = [v * (v + 1.0) * 0.5 for v in n]
         spin = [
-            sum(scalars[slots["w"] + s * TRANSMONS + k] * triangle[k] for k in range(TRANSMONS))
+            sum(weights[s][k] * triangle[k] for k in range(TRANSMONS))
             for s in range(STEPS)
         ]
         if which == 0:
@@ -394,7 +446,7 @@
         decay = 0.0
         for k in range(TRANSMONS):
             gap = digit(row_index, k).astype(jnp.float32) - digit(col_index, k).astype(jnp.float32)
-            decay = decay + scalars[slots["d"] + k] * (gap * gap)
+            decay = decay + dephase[k] * (gap * gap)
         size = jnp.exp(-0.5 * spans[which] * decay)
         row_cos, row_sin = row_waves
         col_cos, col_sin = col_waves
@@ -534,17 +586,21 @@
         for copy in copies:
             copy.wait()
 
-    build_row_table(pre_table, 0)
+    pl.semaphore_wait(barrier, members + phases - 2)
+    tick_copies = send_ticks()
+    handed = hand(state, following, before, 0)
     build_dense(first_high, first_low, 0, True)
     build_sides(0)
-    pl.semaphore_wait(barrier, members + 1)
+    for copy in tick_copies:
+        copy.wait()
+    set_weights()
+    build_row_table(pre_table, 0)
 
     def read_state(where):
         real, imag = state[0, :, where], state[1, :, where]
         return real + imag, real - imag
 
     copies = outbound(read_state, 1.0, pre_table, 0, first_high, first_low, 0)
-    handed = hand(state, following, before, 0)
     build_sides(1)
     build_mid_table()
     build_dense(second_high, second_low, 1, False)
@@ -586,35 +642,6 @@
     phases, members = lax.axis_size("phase"), lax.axis_size("row")
     current = linkage[:, 0]
     rows, order = current.shape[1], current.shape[2]
-    mine = lax.axis_index("phase")
-    total = jnp.sum(ticks, axis=1, dtype=jnp.int32)
-    start = jnp.zeros((1,), jnp.int32)
-    for distance in range(1, phases):
-        other = shifted(total, "phase", distance)
-        start = start + jnp.where(mine >= distance, other, 0)
-    tau = ticks[0].astype(jnp.float32)
-    clock = (start + jnp.cumsum(ticks[0]) - ticks[0]).astype(jnp.float32)
-    spin = (clock + 0.5 * tau)[:, None] * detuning[None, :]
-    onehot = (segments[0][:, None] == jnp.arange(SEGMENTS, dtype=jnp.int32)[None, :])
-    theta = jnp.sum(jnp.where(onehot[:, :, None, None], pulse[None], 0.0), axis=1)
-    cosine, sine = jnp.cos(theta), jnp.sin(theta)
-    one = jnp.ones_like(cosine[:, :, 0])
-    cells = []
-    for i in range(LEVELS):
-        for j in range(LEVELS):
-            if i > j + 1:
-                cells.append(0.0 * one)
-            elif i == j + 1:
-                cells.append(sine[:, :, j])
-            else:
-                cell = one if i == 0 else cosine[:, :, i - 1]
-                for m in range(i, j):
-                    cell = cell * -sine[:, :, m]
-                cells.append(cell if j == LEVELS - 1 else cell * cosine[:, :, j])
-    quads = jnp.stack(cells, axis=-1)
-    scalars = jnp.concatenate(
-        [quads.reshape(-1), spin.reshape(-1), tau, level_shift, coupling, dephase]
-    )
     lanes = order // members
     full = (2, rows, order)
     one_way = (2, members, rows, lanes)
@@ -623,9 +650,10 @@
     result = pl.pallas_call(
         functools.partial(kernel, phases, members),
         out_shape=jax.ShapeDtypeStruct(full, jnp.float32),
-        in_specs=[pl.BlockSpec(memory_space=pltpu.SMEM), vmem],
+        in_specs=[pl.BlockSpec(memory_space=pltpu.SMEM)] * 6 + [vmem] * 3,
         out_specs=vmem,
         scratch_shapes=[
+            pltpu.VMEM((phases, 1, STEPS), jnp.int32),
             pltpu.VMEM(full, jnp.float32),
             pltpu.VMEM(full, jnp.float32),
             pltpu.VMEM(full, jnp.float32),
@@ -649,11 +677,12 @@
             pltpu.SemaphoreType.DMA((4, members)),
             pltpu.SemaphoreType.DMA((2, 2)),
             pltpu.SemaphoreType.DMA((4,)),
+            pltpu.SemaphoreType.DMA((2, phases)),
         ],
         compiler_params=pltpu.CompilerParams(
             collective_id=0, has_side_effects=True, vmem_limit_bytes=56 * 1024 * 1024
         ),
-    )(scalars, current)
+    )(ticks, segments, detuning, level_shift, coupling, dephase, ticks, pulse, current)
     return result[:, None]
 
 

time: 106 us -> 97.9 us (0.924)
  local copies, waits for them, and re-layouts: 6.65 us -> 3.78 us
  other arithmetic: 2.4 us -> 0 us
  between operations: 1.91 us -> 0.01 us
  starting transfers between devices: 1.75 us -> 0 us
    ppermute x3 -> x0, starting transfers between devices: 1.75 us -> none  [shifted(): return lax.ppermute(block, axis, route)]
    convert_element_type x1 -> x0, other arithmetic: 1.31 us -> none  [fused(): tau = ticks[0].astype(jnp.float32)]
    unnamed x13 -> x2, local copies, waits for them, and re-layouts: 4.3 us -> 3.78 us
  transfers between devices with their start and end apart: 3 -> 0, of which waited for: 0 -> 0; matrix products, arithmetic and copies ran while one was open for 2% -> 0% of each run, Pallas kernels for 0% -> 0%
where the time goes in v1:
time: 97.9 us; the launch traced here: 97.6 us
  Pallas kernels  93.9 us (96%)
  local copies, waits for them, and re-layouts  3.78 us (4%)
    pallas_call x1, Pallas kernels, fused(): pl.pallas_call(functools.partial(kernel, phases, members), out_shape=jax....  93.9 us
    unnamed x2, local copies, waits for them, and re-layouts  3.78 us

profile of v1, /device:TPU:10, one launch (start us, length us, event | category | flops | bytes accessed | tf_op | source)
XLA Modules:
  0.0 97.6 jit_solution(1589811161861207982)
XLA Ops:
  0.0 1.5 %copy.9.pulse = f32[32,5,3]{2,1,0:T(8,128)} copy(f32[32,5,3]{0,2,1:T(4,128)} %param.9) | data formatting | bytes 3840 | tf_op args[1]
  1.5 93.9 %shard_map.82 = f32[2,128,1024]{2,1,0:T(8,128)} custom-call(s32[1,2]{1,0:T(1,128)} %tick_row.1, s32[1,2]{1,0:T(1,128)} %segments.1, f32[5]{0:T(128)} %detuning.1, f32[5]{0:T(128)} %level_shift.1, f32[4]{0:T(128)} %coupling.1, f32[5]{0:T(128)} %dephase.1, s32[1,2]{1,0:T(1,128)} %tick_row.1, f32[32,5,3]{2,1,0:T(8,128)} %copy.9.pulse, f32[2,128,1024]{2,1,0:T(8,128)} %bitcast.5), custom_call_target="tpu_custom_call" | custom-call | tf_op jit(solution)/shard_map/pallas_call | solution.py:650
  95.3 2.3 %copy.12 = f32[2,1,128,1024]{3,2,1,0:T(8,128)} copy(f32[2,1,128,1024]{3,2,1,0:T(8,128)} %bitcast.4) | data formatting | bytes 2097152

commit v2 on v1

--- a/solution.py
+++ b/solution.py
@@ -528,13 +528,13 @@
                 for b in range(members):
                     for part in range(per):
                         start = part * trail + b * count
-                        send_one[trip // 2, (b + block) % members, start : start + count, :] = moved[
+                        send_one[trip // 3, (b + block) % members, start : start + count, :] = moved[
                             start : start + count, inner * lanes : (inner + 1) * lanes
                         ]
-        return exchange(send_one.at[trip // 2], receive_one.at[trip // 2], trip)
+        return exchange(send_one.at[trip // 3], receive_one.at[trip // 3], trip)
 
     def middle(sign, first_side, second_side, trip):
-        went = trip // 2
+        went = trip // 3
         for block in range(members):
             pieces = []
             for a in range(lead):
@@ -542,45 +542,48 @@
                 pieces.append(receive_one[went, a // per, start : start + count, :])
             value = jnp.concatenate(pieces, axis=0)
             turned[block] = dot3(sides[first_side], sides[first_side + 1], *split(value))
-        for block in range(members):
-            other = lax.rem(me + members - block, members)
-            straight = turned[block]
-            crossed = turned[other].T
-            real, imag = mid_table[0, block], sign * mid_table[1, block]
-            for kind, value in enumerate(
-                (real * straight + imag * crossed, real * crossed - imag * straight)
-            ):
+        trips = []
+        for kind in range(2):
+            for block in range(members):
+                other = lax.rem(me + members - block, members)
+                straight = turned[block]
+                crossed = turned[other].T
+                real, imag = mid_table[0, block], sign * mid_table[1, block]
+                if kind == 0:
+                    value = real * straight + imag * crossed
+                else:
+                    value = real * crossed - imag * straight
                 moved = dot3(sides[second_side], sides[second_side + 1], *split(value))
                 for a in range(lead):
                     start = (a % per) * trail + block * count
-                    send_two[went, a // per, kind, start : start + count, :] = moved[
+                    send_two[went, kind, a // per, start : start + count, :] = moved[
                         a * count : (a + 1) * count, :
                     ]
-        return exchange(send_two.at[went], receive_two.at[went], trip)
-
-    def inbound(side, high, low, trip):
-        went = trip // 2
+            trips.append(
+                exchange(send_two.at[went, kind], receive_two.at[went, kind], trip + kind)
+            )
+        return trips
+
+    def inbound(side, high, low, went, kind):
         for block in range(members):
-            for kind in range(2):
-                pieces = []
-                for part in range(per):
-                    for b in range(members):
-                        start = part * trail + b * count
-                        pieces.append(
-                            receive_two[went, (b + block) % members, kind, start : start + count, :]
-                        )
-                upper, lower = split(jnp.concatenate(pieces, axis=0))
-                where = (slice(kind * rows, (kind + 1) * rows), slice(block * lanes, (block + 1) * lanes))
-                gathered_high[where] = upper
-                gathered_low[where] = lower
+            pieces = []
+            for part in range(per):
+                for b in range(members):
+                    start = part * trail + b * count
+                    pieces.append(
+                        receive_two[went, kind, (b + block) % members, start : start + count, :]
+                    )
+            upper, lower = split(jnp.concatenate(pieces, axis=0))
+            where = (slice(0, rows), slice(block * lanes, (block + 1) * lanes))
+            gathered_high[where] = upper
+            gathered_low[where] = lower
         wide = 2 * width
         for chunk in range(order // wide):
             where = pl.ds(chunk * wide, wide)
-            moved = dot3(gathered_high[...], gathered_low[...], high[where, :], low[where, :], 1)
-            for kind in range(2):
-                halfway[kind, :, where] = dot3(
-                    sides[side], sides[side + 1], *split(moved[kind * rows : (kind + 1) * rows])
-                )
+            moved = dot3(
+                gathered_high[0:rows, :], gathered_low[0:rows, :], high[where, :], low[where, :], 1
+            )
+            halfway[kind, :, where] = dot3(sides[side], sides[side + 1], *split(moved))
 
     def wait(copies):
         for copy in copies:
@@ -606,10 +609,11 @@
     build_dense(second_high, second_low, 1, False)
     build_row_table(post_table, 2)
     wait(copies)
-    copies = middle(1.0, 2, 10, 1)
+    trips = middle(1.0, 2, 10, 1)
+    for kind in range(2):
+        wait(trips[kind])
+        inbound(8, second_high, second_low, 0, kind)
     handed.wait()
-    wait(copies)
-    inbound(8, second_high, second_low, 1)
     for chunk in range(order // width):
         where = pl.ds(chunk * width, width)
         straight, crossed = halfway[0, :, where], halfway[1, :, where]
@@ -621,13 +625,14 @@
     def read_mismatch(where):
         return mismatch[0, :, where], mismatch[1, :, where]
 
-    copies = outbound(read_mismatch, -1.0, post_table, 12, second_high, second_low, 2)
+    copies = outbound(read_mismatch, -1.0, post_table, 12, second_high, second_low, 3)
     handed = hand(mismatch, earlier, after, 1)
     wait(copies)
-    copies = middle(-1.0, 14, 6, 3)
+    trips = middle(-1.0, 14, 6, 4)
+    for kind in range(2):
+        wait(trips[kind])
+        inbound(4, first_high, first_low, 1, kind)
     handed.wait()
-    wait(copies)
-    inbound(4, first_high, first_low, 3)
     for chunk in range(order // width):
         where = pl.ds(chunk * width, width)
         straight, crossed = halfway[0, :, where], halfway[1, :, where]
@@ -645,7 +650,7 @@
     lanes = order // members
     full = (2, rows, order)
     one_way = (2, members, rows, lanes)
-    two_way = (2, members, 2, rows, lanes)
+    two_way = (2, 2, members, rows, lanes)
     vmem = pl.BlockSpec(memory_space=pltpu.VMEM)
     result = pl.pallas_call(
         functools.partial(kernel, phases, members),
@@ -666,17 +671,17 @@
             pltpu.VMEM((2, members, lanes, lanes), jnp.float32),
             pltpu.VMEM(full, jnp.float32),
             pltpu.VMEM((members, lanes, lanes), jnp.float32),
-            pltpu.VMEM((2 * rows, order), jnp.bfloat16),
-            pltpu.VMEM((2 * rows, order), jnp.bfloat16),
+            pltpu.VMEM((rows, order), jnp.bfloat16),
+            pltpu.VMEM((rows, order), jnp.bfloat16),
             pltpu.VMEM(full, jnp.float32),
             pltpu.VMEM(one_way, jnp.float32),
             pltpu.VMEM(one_way, jnp.float32),
             pltpu.VMEM(two_way, jnp.float32),
             pltpu.VMEM(two_way, jnp.float32),
-            pltpu.SemaphoreType.DMA((4, members)),
-            pltpu.SemaphoreType.DMA((4, members)),
+            pltpu.SemaphoreType.DMA((6, members)),
+            pltpu.SemaphoreType.DMA((6, members)),
             pltpu.SemaphoreType.DMA((2, 2)),
-            pltpu.SemaphoreType.DMA((4,)),
+            pltpu.SemaphoreType.DMA((6,)),
             pltpu.SemaphoreType.DMA((2, phases)),
         ],
         compiler_params=pltpu.CompilerParams(

time: 97.9 us -> 100 us (1.021)
  Pallas kernels: 93.9 us -> 95.6 us
    pallas_call x1, Pallas kernels: 93.9 us -> 95.6 us  [fused(): pl.pallas_call(functools.partial(kernel, phases, members), out_shape=jax....]
where the time goes in v2:
time: 100 us; the launch traced here: 99.4 us
  Pallas kernels  95.6 us (96%)
  local copies, waits for them, and re-layouts  3.78 us (4%)
    pallas_call x1, Pallas kernels, fused(): pl.pallas_call(functools.partial(kernel, phases, members), out_shape=jax....  95.6 us
    unnamed x2, local copies, waits for them, and re-layouts  3.78 us

profile of v2, /device:TPU:10, one launch (start us, length us, event | category | flops | bytes accessed | tf_op | source)
XLA Modules:
  0.0 99.4 jit_solution(10352456651843300258)
XLA Ops:
  0.0 1.5 %copy.9.pulse = f32[32,5,3]{2,1,0:T(8,128)} copy(f32[32,5,3]{0,2,1:T(4,128)} %param.9) | data formatting | bytes 3840 | tf_op args[1]
  1.5 95.6 %shard_map.82 = f32[2,128,1024]{2,1,0:T(8,128)} custom-call(s32[1,2]{1,0:T(1,128)} %tick_row.1, s32[1,2]{1,0:T(1,128)} %segments.1, f32[5]{0:T(128)} %detuning.1, f32[5]{0:T(128)} %level_shift.1, f32[4]{0:T(128)} %coupling.1, f32[5]{0:T(128)} %dephase.1, s32[1,2]{1,0:T(1,128)} %tick_row.1, f32[32,5,3]{2,1,0:T(8,128)} %copy.9.pulse, f32[2,128,1024]{2,1,0:T(8,128)} %bitcast.5), custom_call_target="tpu_custom_call" | custom-call | tf_op jit(solution)/shard_map/pallas_call | solution.py:655
  97.1 2.3 %copy.12 = f32[2,1,128,1024]{3,2,1,0:T(8,128)} copy(f32[2,1,128,1024]{3,2,1,0:T(8,128)} %bitcast.4) | data formatting | bytes 2097152
